TPU v7x, 32 devices: a whole 2x2x4 slice. The times are simulated.
32 devices in a mesh: dp: 8 (over z, core), mp: 4 (over y, x).
Axes of the slice: x: 2, y: 2, z: 4, core: 2. Of those that a mesh axis runs over, the one named last changes fastest.
Arguments:
- tokens: bfloat16 [12288, 2048], P(('dp', 'mp')), may hold values from -6 to 6
- segment_ids: int32 [16, 768], P('dp'), may hold values from 0 to 5, never falling along the last dimension, each value on 1 to 256 neighbouring positions
- query_weight: bfloat16 [2048, 2048], P(None, 'mp'), may hold values from -0.125 to 0.125
- key_weight: bfloat16 [2048, 2048], P(None, 'mp'), may hold values from -0.125 to 0.125
- value_weight: bfloat16 [2048, 2048], P(None, 'mp'), may hold values from -0.125 to 0.125
- out_weight: bfloat16 [2048, 2048], P('mp'), may hold values from -0.75 to 0.75
- up_weight: bfloat16 [2048, 8192], P(None, 'mp'), may hold values from -0.125 to 0.125
- down_weight: bfloat16 [8192, 2048], P('mp'), may hold values from -0.0625 to 0.0625
- attn_gain: float32 [2048], replicated, may hold values from 0.5 to 1.5
- mlp_gain: float32 [2048], replicated, may hold values from 0.5 to 1.5
- out_cotangent: bfloat16 [12288, 2048], P(('dp', 'mp')), may hold values from -18 to 18
Outputs:
- layer_output: bfloat16 [12288, 2048], P(('dp', 'mp'))
- tokens_grad: float32 [12288, 2048], P(('dp', 'mp'))
- query_weight_grad: float32 [2048, 2048], P('dp', 'mp')
- key_weight_grad: float32 [2048, 2048], P('dp', 'mp')
- value_weight_grad: float32 [2048, 2048], P('dp', 'mp')
- out_weight_grad: float32 [2048, 2048], P('mp', 'dp')
- up_weight_grad: float32 [2048, 8192], P('dp', 'mp')
- down_weight_grad: float32 [8192, 2048], P('mp', 'dp')
- attn_gain_grad: float32 [2048], replicated
- mlp_gain_grad: float32 [2048], replicated
Inputs may be any that keep to these rules, and one draw needn't show every extreme that they name: `segment_ids`: within each packed sequence the clip numbers never fall; each clip covers 1 to 256 tokens, and some clip covers exactly 256.
All inputs are finite; a program needn't handle non-finite values.
Results may differ from a plain program's by a relative error of at most 0.02.
Values may be sent and summed in bfloat16 or wider, within the bound.
A program may use at most 192 MiB of HBM per device.

v0:
```python
import math
import jax
import jax.numpy as jnp
from jax import lax
from jax.sharding import PartitionSpec as P

HEAD_DIM = 128
epsilon = 1e-05
masked_score = -1e30


def norm_rows(values, gain):
    centre = jnp.mean(values, axis=-1, keepdims=True)
    centred = values - centre
    spread = jnp.mean(centred * centred, axis=-1, keepdims=True)
    return centred * lax.rsqrt(spread + epsilon) * gain


def gelu_tanh(values):
    return jax.nn.gelu(values, approximate=True)


def block_allowed(segment):
    position = jnp.arange(segment.shape[0])
    return (position[None, :] <= position[:, None]) & (segment[:, None] == segment[None, :])


def rows_times(left_rows, right_matrix):
    return jnp.dot(left_rows, right_matrix, preferred_element_type=jnp.float32)


def rows_times_back(left_rows, right_matrix):
    return lax.dot_general(
        left_rows, right_matrix, (((1,), (1,)), ((), ())), preferred_element_type=jnp.float32
    )


def attn_input_back(
    queries_grad, keys_grad, values_grad, query_weight, key_weight, value_weight, score_scale
):
    total_grad = rows_times_back(queries_grad, query_weight) * score_scale
    total_grad = total_grad + rows_times_back(keys_grad, key_weight)
    return total_grad + rows_times_back(values_grad, value_weight)


def attend_forward(packed):
    queries, keys_in, values_in, segment = packed
    scores = jnp.einsum("qhd,khd->hqk", queries, keys_in, preferred_element_type=jnp.float32)
    scores = jnp.where(block_allowed(segment)[None], scores, masked_score)
    row_max = jnp.max(scores, axis=-1, keepdims=True)
    expanded = jnp.exp(scores - row_max)
    row_total = jnp.sum(expanded, axis=-1, keepdims=True)
    probs_low = (expanded / row_total).astype(jnp.bfloat16)
    context = jnp.einsum("hqk,khd->qhd", probs_low, values_in, preferred_element_type=jnp.float32)
    return (context.astype(jnp.bfloat16), (row_max + jnp.log(row_total))[:, :, 0])


def attend_backward(packed):
    queries, keys_in, values_in, segment, context_grad, log_total = packed
    scores = jnp.einsum("qhd,khd->hqk", queries, keys_in, preferred_element_type=jnp.float32)
    scores = jnp.where(block_allowed(segment)[None], scores, masked_score)
    attn_probs = jnp.exp(scores - log_total[:, :, None])
    probs_grad = jnp.einsum(
        "qhd,khd->hqk", context_grad, values_in, preferred_element_type=jnp.float32
    )
    values_grad = jnp.einsum(
        "hqk,qhd->khd",
        attn_probs.astype(jnp.bfloat16),
        context_grad,
        preferred_element_type=jnp.float32,
    )
    inner_sum = jnp.sum(attn_probs * probs_grad, axis=-1, keepdims=True)
    scores_grad = (attn_probs * (probs_grad - inner_sum)).astype(jnp.bfloat16)
    queries_grad = jnp.einsum(
        "hqk,khd->qhd", scores_grad, keys_in, preferred_element_type=jnp.float32
    )
    keys_grad = jnp.einsum("hqk,qhd->khd", scores_grad, queries, preferred_element_type=jnp.float32)
    return (
        queries_grad.astype(jnp.bfloat16),
        keys_grad.astype(jnp.bfloat16),
        values_grad.astype(jnp.bfloat16),
    )


def local(
    tokens,
    segment_ids,
    query_weight,
    key_weight,
    value_weight,
    out_weight,
    up_weight,
    down_weight,
    attn_gain,
    mlp_gain,
    out_cotangent,
):
    seq_count, seq_length = segment_ids.shape
    group_rows = seq_count * seq_length
    head_count = query_weight.shape[1] // HEAD_DIM
    score_scale = 1.0 / math.sqrt(HEAD_DIM)
    shaped = (seq_count, seq_length, head_count, HEAD_DIM)
    flat_shape = (group_rows, head_count * HEAD_DIM)
    residual_in = tokens.astype(jnp.float32)
    normed_attn, attn_norm_back = jax.vjp(norm_rows, residual_in, attn_gain)
    gathered_attn = lax.all_gather(normed_attn.astype(jnp.bfloat16), "mp", axis=0, tiled=True)
    queries = (
        jnp.dot(gathered_attn, query_weight, preferred_element_type=jnp.float32) * score_scale
    ).astype(jnp.bfloat16)
    keys_all = jnp.dot(gathered_attn, key_weight, preferred_element_type=jnp.float32).astype(
        jnp.bfloat16
    )
    values_all = jnp.dot(gathered_attn, value_weight, preferred_element_type=jnp.float32).astype(
        jnp.bfloat16
    )
    queries_seq = queries.reshape(shaped)
    keys_seq = keys_all.reshape(shaped)
    values_seq = values_all.reshape(shaped)
    context, log_total = lax.map(attend_forward, (queries_seq, keys_seq, values_seq, segment_ids))
    context_flat = context.reshape(flat_shape)
    attn_rows = lax.psum_scatter(
        rows_times(context_flat, out_weight).astype(jnp.bfloat16),
        "mp",
        scatter_dimension=0,
        tiled=True,
    ).astype(jnp.float32)
    residual_mid = residual_in + attn_rows
    normed_mlp, mlp_norm_back = jax.vjp(norm_rows, residual_mid, mlp_gain)
    gathered_mlp = lax.all_gather(normed_mlp.astype(jnp.bfloat16), "mp", axis=0, tiled=True)
    pre_act = jnp.dot(gathered_mlp, up_weight, preferred_element_type=jnp.float32)
    activated, gelu_back = jax.vjp(gelu_tanh, pre_act)
    hidden = activated.astype(jnp.bfloat16)
    mlp_rows = lax.psum_scatter(
        rows_times(hidden, down_weight).astype(jnp.bfloat16), "mp", scatter_dimension=0, tiled=True
    ).astype(jnp.float32)
    layer_output = (residual_mid + mlp_rows).astype(jnp.bfloat16)
    cotangent_all = lax.all_gather(out_cotangent, "mp", axis=0, tiled=True)
    down_weight_grad = jnp.einsum(
        "rf,rd->fd", hidden, cotangent_all, preferred_element_type=jnp.float32
    )
    hidden_grad = lax.dot_general(
        cotangent_all, down_weight, (((1,), (1,)), ((), ())), preferred_element_type=jnp.float32
    )
    pre_grad = gelu_back(hidden_grad)[0].astype(jnp.bfloat16)
    up_weight_grad = jnp.einsum(
        "rd,rf->df", gathered_mlp, pre_grad, preferred_element_type=jnp.float32
    )
    normed_mlp_grad = lax.psum_scatter(
        rows_times_back(pre_grad, up_weight).astype(jnp.bfloat16),
        "mp",
        scatter_dimension=0,
        tiled=True,
    ).astype(jnp.float32)
    middle_back, mlp_gain_grad = mlp_norm_back(normed_mlp_grad)
    middle_grad = out_cotangent.astype(jnp.float32) + middle_back
    middle_all_grad = lax.all_gather(middle_grad.astype(jnp.bfloat16), "mp", axis=0, tiled=True)
    out_weight_grad = jnp.einsum(
        "rc,rd->cd", context_flat, middle_all_grad, preferred_element_type=jnp.float32
    )
    context_grad = lax.dot_general(
        middle_all_grad, out_weight, (((1,), (1,)), ((), ())), preferred_element_type=jnp.float32
    ).astype(jnp.bfloat16)
    queries_grad, keys_grad, values_grad = lax.map(
        attend_backward,
        (queries_seq, keys_seq, values_seq, segment_ids, context_grad.reshape(shaped), log_total),
    )
    queries_grad = queries_grad.reshape(flat_shape)
    keys_grad = keys_grad.reshape(flat_shape)
    values_grad = values_grad.reshape(flat_shape)
    query_weight_grad = (
        jnp.einsum("rd,rc->dc", gathered_attn, queries_grad, preferred_element_type=jnp.float32)
        * score_scale
    )
    key_weight_grad = jnp.einsum(
        "rd,rc->dc", gathered_attn, keys_grad, preferred_element_type=jnp.float32
    )
    value_weight_grad = jnp.einsum(
        "rd,rc->dc", gathered_attn, values_grad, preferred_element_type=jnp.float32
    )
    normed_attn_grad = lax.psum_scatter(
        attn_input_back(
            queries_grad,
            keys_grad,
            values_grad,
            query_weight,
            key_weight,
            value_weight,
            score_scale,
        ).astype(jnp.bfloat16),
        "mp",
        scatter_dimension=0,
        tiled=True,
    ).astype(jnp.float32)
    token_back, attn_gain_grad = attn_norm_back(normed_attn_grad)
    tokens_grad = middle_grad + token_back
    attn_gain_grad, mlp_gain_grad = lax.psum((attn_gain_grad, mlp_gain_grad), ("dp", "mp"))
    (
        query_weight_grad,
        key_weight_grad,
        value_weight_grad,
        out_weight_grad,
        up_weight_grad,
        down_weight_grad,
    ) = (
        lax.psum_scatter(
            query_weight_grad.astype(jnp.bfloat16), "dp", scatter_dimension=0, tiled=True
        ).astype(jnp.float32),
        lax.psum_scatter(
            key_weight_grad.astype(jnp.bfloat16), "dp", scatter_dimension=0, tiled=True
        ).astype(jnp.float32),
        lax.psum_scatter(
            value_weight_grad.astype(jnp.bfloat16), "dp", scatter_dimension=0, tiled=True
        ).astype(jnp.float32),
        lax.psum_scatter(
            out_weight_grad.astype(jnp.bfloat16), "dp", scatter_dimension=1, tiled=True
        ).astype(jnp.float32),
        lax.psum_scatter(
            up_weight_grad.astype(jnp.bfloat16), "dp", scatter_dimension=0, tiled=True
        ).astype(jnp.float32),
        lax.psum_scatter(
            down_weight_grad.astype(jnp.bfloat16), "dp", scatter_dimension=1, tiled=True
        ).astype(jnp.float32),
    )
    return (
        layer_output,
        tokens_grad,
        query_weight_grad,
        key_weight_grad,
        value_weight_grad,
        out_weight_grad,
        up_weight_grad,
        down_weight_grad,
        attn_gain_grad,
        mlp_gain_grad,
    )


def solution(mesh):
    return jax.shard_map(
        local,
        mesh=mesh,
        in_specs=(
            P(("dp", "mp"), None),
            P("dp", None),
            P(None, "mp"),
            P(None, "mp"),
            P(None, "mp"),
            P("mp", None),
            P(None, "mp"),
            P("mp", None),
            P(),
            P(),
            P(("dp", "mp"), None),
        ),
        out_specs=(
            P(("dp", "mp"), None),
            P(("dp", "mp"), None),
            P("dp", "mp"),
            P("dp", "mp"),
            P("dp", "mp"),
            P("mp", "dp"),
            P("dp", "mp"),
            P("mp", "dp"),
            P(),
            P(),
        ),
        check_vma=False,
    )
```

profile of v0, /device:TPU:0, one launch (start us, length us, event | category | flops | bytes accessed | tf_op | source)
XLA Modules:
  0.0 1105.6 jit_solution(7210589673843302547)
XLA Ops:
  14.0 73.0 %all-gather.5.cloned.1.call-done = bf16[1536,2048]{1,0:T(8,128)(2,1)} async-done(((bf16[384,2048]{1,0:T(8,128)(2,1)}), bf16[1536,2048]{1,0:T(8,128)(2,1)}) %all-gather.5.cloned.1.call-update) | async-done | bytes 6291472 | tf_op jit(solution)/shard_map/all_gather | solution.py:106
  87.0 8.0 convolution_convert_fusion.11
  94.9 3.7 reshape.216
  101.6 7.3 fusion.63
  115.3 7.3 convolution_convert_fusion.12
  127.6 28.2 %while.26 = (s32[]{:T(128)}, bf16[2,768,4,128]{3,2,1,0:T(4,128)(2,1)}, f32[2,4,768]{2,1,0:T(4,128)S(1)}, bf16[2,768,4,128]{3,2,1,0:T(4,128)(2,1)}, s32[2,768]{1,...) while((s32[]{:T(128)}, ...), condition=%wide.region_5.6_spmd, body=%wide.region_2.5_spmd.sunk | while | flops 1231352832 | bytes 43362440 | solution.py:119
  135.4 3.6 fusion.137
  149.5 3.6 fusion.137
  155.8 7.2 convolution_convert_fusion.6
  163.8 69.6 %reduce-scatter.11.cloned.1.call-done = bf16[384,2048]{1,0:T(8,128)(2,1)} async-done(((bf16[1536,2048]{1,0:T(8,128)(2,1)}), bf16[384,2048]{1,0:T(8,128)(2,1)}) %reduce-scatter.11.cloned.1.call-update) | async-done | bytes 1572880 | tf_op jit(solution)/shard_map/reduce_scatter | solution.py:121
  238.9 66.6 %all-gather.9.cloned.1.call-done = bf16[1536,2048]{1,0:T(8,128)(2,1)} async-done(((bf16[384,2048]{1,0:T(8,128)(2,1)}), bf16[1536,2048]{1,0:T(8,128)(2,1)}) %all-gather.9.cloned.1.call-update) | async-done | bytes 6291472 | tf_op jit(solution)/shard_map/all_gather | solution.py:137
  305.5 19.1 %fusion.89 = f32[1536,2048]{1,0:T(8,128)} fusion(bf16[1536,2048]{1,0:T(8,128)(2,1)} %all-gather.9.cloned.1.call-done, bf16[2048,2048]{1,0:T(8,128)(2,1)} %param.22), kind=kOutput, calls=%fused_computation.146 | convolution fusion | flops 12884901888 | bytes 27262976 | tf_op jit(solution)/shard_map/dot_general | solution.py:141
  324.5 53.4 %all-gather.7.cloned.1.call-done = bf16[1536,2048]{1,0:T(8,128)(2,1)} async-done(((bf16[384,2048]{1,0:T(8,128)(2,1)}), bf16[1536,2048]{1,0:T(8,128)(2,1)}) %all-gather.7.cloned.1.call-update) | async-done | bytes 6291472 | tf_op jit(solution)/shard_map/all_gather | solution.py:129
  377.9 29.6 %fusion.48 = (bf16[1536,2048]{1,0:T(8,128)(2,1)}, f32[1536,2048]{1,0:T(8,128)}) fusion(f32[1536,2048]{1,0:T(8,128)} %fusion.89, bf16[1536,2048]{1,0:T(8,128)(2,1)} %all-gather.7.cloned.1.call-done, bf16[2048,2048]{1,0:T(8,128)(2,1)} %param.21), kind=kOutput, calls=%fused_computation.68 | convolution fusion | flops 12947816448 | bytes 46137344 | tf_op jit(solution)/shard_map/dot_general | solution.py:130
  407.5 19.1 %convolution_convert_fusion.4 = bf16[1536,2048]{1,0:T(8,128)(2,1)} fusion(bf16[1536,2048]{1,0:T(8,128)(2,1)} %get-tuple-element.190, bf16[2048,2048]{1,0:T(8,128)(2,1)} %param.21), kind=kOutput, calls=%fused_computation.73 | convolution fusion | flops 12888047616 | bytes 20971520 | tf_op jit(solution)/shard_map/dot_general | solution.py:33
  426.7 20.5 %convolution_convert_fusion.5 = bf16[1536,2048]{1,0:T(8,128)(2,1)} fusion(bf16[2048,2048]{1,0:T(8,128)(2,1)} %param.22, f32[1536,2048]{1,0:T(8,128)} %get-tuple-element.191), kind=kOutput, calls=%fused_computation.74 | convolution fusion | flops 12916359168 | bytes 27262976 | tf_op jit(solution)/shard_map/dot_general | solution.py:29
  447.3 49.7 %reduce-scatter.15.cloned.1.call-done = bf16[384,2048]{1,0:T(8,128)(2,1)} async-done(((bf16[1536,2048]{1,0:T(8,128)(2,1)}), bf16[384,2048]{1,0:T(8,128)(2,1)}) %reduce-scatter.15.cloned.1.call-update) | async-done | bytes 1572880 | tf_op jit(solution)/shard_map/reduce_scatter | solution.py:148
  497.0 4.4 fusion.59
  501.4 68.7 %reduce-scatter.13.cloned.1.call-done = bf16[384,2048]{1,0:T(8,128)(2,1)} async-done(((bf16[1536,2048]{1,0:T(8,128)(2,1)}), bf16[384,2048]{1,0:T(8,128)(2,1)}) %reduce-scatter.13.cloned.1.call-update) | async-done | bytes 1572880 | tf_op jit(solution)/shard_map/reduce_scatter | solution.py:133
  570.1 5.5 fusion.88
  578.9 19.6 %convolution_convert_fusion.3 = bf16[2048,2048]{1,0:T(8,128)(2,1)} fusion(bf16[1536,2048]{1,0:T(8,128)(2,1)} %all-gather.7.cloned.1.call-done, bf16[1536,2048]{1,0:T(8,128)(2,1)} %get-tuple-element.190), kind=kOutput, calls=%fused_computation.72 | convolution fusion | flops 12889096192 | bytes 20971520 | tf_op jit(solution)/shard_map/rd,rf->df/dot_general | solution.py:145
  598.5 22.5 %convolution_convert_fusion.2 = bf16[2048,2048]{1,0:T(8,128)(2,1)} fusion(bf16[1536,2048]{1,0:T(8,128)(2,1)} %all-gather.9.cloned.1.call-done, f32[1536,2048]{1,0:T(8,128)} %get-tuple-element.191), kind=kOutput, calls=%fused_computation.71 | convolution fusion | flops 12917407744 | bytes 27262976 | tf_op jit(solution)/shard_map/rf,rd->fd/dot_general | solution.py:138
  621.1 28.0 %all-gather.11.cloned.1.call-done = bf16[1536,2048]{1,0:T(8,128)(2,1)} async-done(((bf16[384,2048]{1,0:T(8,128)(2,1)}), bf16[1536,2048]{1,0:T(8,128)(2,1)}) %all-gather.11.cloned.1.call-update) | async-done | bytes 6291472 | tf_op jit(solution)/shard_map/all_gather | solution.py:156
  649.1 7.8 convolution_convert_fusion.10
  657.0 3.7 reshape.218
  660.6 8.1 convolution_convert_fusion.7
  673.6 99.9 %while.27 = (s32[]{:T(128)}, bf16[2,768,4,128]{3,2,1,0:T(4,128)(2,1)}, bf16[2,768,4,128]{3,2,1,0:T(4,128)(2,1)}, bf16[2,768,4,128]{3,2,1,0:T(4,128)(2,1)}, bf16[...) while((s32[]{:T(128)}, ...), condition=%wide.region_15.16_spmd, body=%wide.region_13.15_spmd.sunk | while | flops 3051156480 | bytes 169179440 | solution.py:163
  679.6 3.6 copy-done.1
  689.0 8.2 multiply_reduce_fusion.3
  697.2 10.9 multiply_convert_fusion.7
  708.1 4.5 fusion.149
  729.1 3.6 copy-done.1
  738.5 8.1 multiply_reduce_fusion.3
  746.6 11.5 %multiply_convert_fusion.7 = bf16[4,768,768]{1,2,0:T(8,128)(2,1)} fusion(f32[4,768,768]{1,2,0:T(8,128)} %get-tuple-element.304, f32[4,768,768]{1,2,0:T(8,128)} %copy-done.1, f32[4,768]{1,0:T(4,128)S(1)} %get-tuple-element.305, f32[4,768]{1,0:T(4,128)S(1)} %dynamic-slice_bitcast_fusion.2, pred[768,768]{0,1:T(8,128)(4,1)S(1)} %fusion.146), kind=kLoop, calls=%fused_computation.21.clone.1 | loop fusion | flops 11796480 | bytes 24207360 | tf_op jit(solution)/shard_map/while/body/eval_jaxpr/convert_element_type | solution.py:73
  758.1 4.4 fusion.149
  773.5 8.1 multiply_convert_fusion.2
  781.7 8.1 convolution_convert_fusion.8
  789.8 8.1 convolution_convert_fusion.9
  798.3 10.2 fusion.72
  808.5 6.5 fusion.69
  815.0 15.8 %add_convert_fusion = bf16[1536,2048]{1,0:T(8,128)(2,1)} fusion(f32[1536,2048]{1,0:T(8,128)} %fusion.69, f32[1536,2048]{1,0:T(8,128)} %fusion.72, bf16[2048,512]{1,0:T(8,128)(2,1)} %param.17, bf16[192,8,4,128]{3,2,1,0:T(4,128)(2,1)} %bitcast.147), kind=kOutput, calls=%fused_computation.69 | convolution fusion | flops 3233808384 | bytes 35127296 | tf_op jit(solution)/shard_map/dot_general | solution.py:33
  836.4 31.3 %reduce-scatter.25.cloned.1.call-done = bf16[512,256]{1,0:T(8,128)(2,1)} async-done(((bf16[512,2048]{1,0:T(8,128)(2,1)}), bf16[512,256]{1,0:T(8,128)(2,1)}) %reduce-scatter.25.cloned.1.call-update) | async-done | bytes 262160 | tf_op jit(solution)/shard_map/reduce_scatter | solution.py:214
  869.4 34.9 %reduce-scatter.19.cloned.1.call-done = bf16[256,512]{1,0:T(8,128)(2,1)} async-done(((bf16[2048,512]{1,0:T(8,128)(2,1)}), bf16[256,512]{1,0:T(8,128)(2,1)}) %reduce-scatter.19.cloned.1.call-update) | async-done | bytes 262160 | tf_op jit(solution)/shard_map/reduce_scatter | solution.py:205
  906.1 34.9 %reduce-scatter.23.cloned.1.call-done = bf16[256,512]{1,0:T(8,128)(2,1)} async-done(((bf16[2048,512]{1,0:T(8,128)(2,1)}), bf16[256,512]{1,0:T(8,128)(2,1)}) %reduce-scatter.23.cloned.1.call-update) | async-done | bytes 262160 | tf_op jit(solution)/shard_map/reduce_scatter | solution.py:211
  942.9 34.9 %reduce-scatter.21.cloned.1.call-done = bf16[256,512]{1,0:T(8,128)(2,1)} async-done(((bf16[2048,512]{1,0:T(8,128)(2,1)}), bf16[256,512]{1,0:T(8,128)(2,1)}) %reduce-scatter.21.cloned.1.call-update) | async-done | bytes 262160 | tf_op jit(solution)/shard_map/reduce_scatter | solution.py:208
  979.6 70.0 %reduce-scatter.17.cloned.1.call-done = bf16[384,2048]{1,0:T(8,128)(2,1)} async-done(((bf16[1536,2048]{1,0:T(8,128)(2,1)}), bf16[384,2048]{1,0:T(8,128)(2,1)}) %reduce-scatter.17.cloned.1.call-update) | async-done | bytes 1572880 | tf_op jit(solution)/shard_map/reduce_scatter | solution.py:180
  1054.0 39.5 %all-reduce = (f32[2048]{0:T(1024)}, f32[2048]{0:T(1024)}) all-reduce(f32[2048]{0:T(1024)S(1)} %get-tuple-element.143, f32[2048]{0:T(1024)S(1)} %copy-done.27), channel_id=1, replica_groups=mesh['dp'=8,'mp'=4] {'dp','mp'}, use_global_device_ids=true, to_apply=%region_26.27 | all-reduce | flops 4096 | bytes 32768 | tf_op jit(solution)/shard_map/psum | solution.py:196
  1093.5 5.1 add_add_fusion.2
  (184 shorter events, 118.7 us)
Async XLA Ops:
  7.2 148.6 %copy-start = (bf16[512,2048]{1,0:T(8,128)(2,1)S(1)}, bf16[512,2048]{1,0:T(8,128)(2,1)}, u32[]{:S(2)}) copy-start(bf16[512,2048]{1,0:T(8,128)(2,1)} %param.20) | copy-start | bytes 6291460
  7.2 5.0 copy-start.20
  7.2 79.8 %all-gather.5.cloned.1.call-start = ((), (), s32[]{:S(2)}) async-start(), calls=%async_computation.10 | async-start | bytes 7864320 | tf_op jit(solution)/shard_map/all_gather | solution.py:106
  7.2 5.0 copy-start.3
  9.1 2.5 copy-start.22
  13.9 219.5 %reduce-scatter.11.cloned.1.call-start = ((), (), s32[]{:S(2)}) async-start(), calls=%async_computation.11 | async-start | bytes 7864320 | tf_op jit(solution)/shard_map/reduce_scatter | solution.py:121
  98.6 2.9 copy-start.14
  112.4 2.9 copy-start.32
  122.6 5.1 copy-start.18
  155.8 7.2 copy-start.16
  163.1 142.4 %all-gather.9.cloned.1.call-start = ((), (), s32[]{:S(2)}) async-start(), calls=%async_computation.14 | async-start | bytes 7864320 | tf_op jit(solution)/shard_map/all_gather | solution.py:137
  163.1 73.9 %copy-start.24 = (f32[2048]{0:T(1024)S(1)}, f32[2048]{0:T(1024)}, u32[]{:S(2)}) copy-start(f32[2048]{0:T(1024)} %param.24) | copy-start | bytes 24580
  163.8 214.1 %all-gather.7.cloned.1.call-start = ((), (), s32[]{:S(2)}) async-start(), calls=%async_computation.12 | async-start | bytes 7864320 | tf_op jit(solution)/shard_map/all_gather | solution.py:129
  233.4 2.5 copy-start.4
  233.4 2.8 copy-start.9
  238.8 258.2 %reduce-scatter.15.cloned.1.call-start = ((), (), s32[]{:S(2)}) async-start(), calls=%async_computation.15 | async-start | bytes 7864320 | tf_op jit(solution)/shard_map/reduce_scatter | solution.py:148
  426.7 143.4 %reduce-scatter.13.cloned.1.call-start = ((), (), s32[]{:S(2)}) async-start(), calls=%async_computation.13 | async-start | bytes 7864320 | tf_op jit(solution)/shard_map/reduce_scatter | solution.py:133
  447.2 201.9 %all-gather.11.cloned.1.call-start = ((), (), s32[]{:S(2)}) async-start(), calls=%async_computation.16 | async-start | bytes 7864320 | tf_op jit(solution)/shard_map/all_gather | solution.py:156
  570.1 7.2 copy-start.13
  578.8 252.0 %reduce-scatter.27.cloned.1.call-start = ((), (), s32[]{:S(2)}) async-start(), calls=%async_computation.22 | async-start | bytes 9437184 | tf_op jit(solution)/shard_map/reduce_scatter | solution.py:217
  598.5 235.2 %reduce-scatter.29.cloned.1.call-start = ((), (), s32[]{:S(2)}) async-start(), calls=%async_computation.23 | async-start | bytes 9437184 | tf_op jit(solution)/shard_map/reduce_scatter | solution.py:220
  621.0 246.6 %reduce-scatter.25.cloned.1.call-start = ((), (), s32[]{:S(2)}) async-start(), calls=%async_computation.21 | async-start | bytes 2359296 | tf_op jit(solution)/shard_map/reduce_scatter | solution.py:214
  668.8 4.8 copy-start.17
  668.8 4.8 copy-start.19
  668.8 235.5 %reduce-scatter.19.cloned.1.call-start = ((), (), s32[]{:S(2)}) async-start(), calls=%async_computation.18 | async-start | bytes 2359296 | tf_op jit(solution)/shard_map/reduce_scatter | solution.py:205
  673.8 4.4 copy-start.6
  673.8 4.4 copy-start.8
  679.6 3.6 copy-start.1
  708.1 4.5 copy-start.2
  708.1 4.6 copy-start.7
  723.3 4.5 copy-start.6
  723.3 4.5 copy-start.8
  729.1 3.6 copy-start.1
  758.1 4.4 copy-start.2
  758.1 4.6 copy-start.7
  781.6 159.5 %reduce-scatter.23.cloned.1.call-start = ((), (), s32[]{:S(2)}) async-start(), calls=%async_computation.20 | async-start | bytes 2359296 | tf_op jit(solution)/shard_map/reduce_scatter | solution.py:211
  789.8 188.0 %reduce-scatter.21.cloned.1.call-start = ((), (), s32[]{:S(2)}) async-start(), calls=%async_computation.19 | async-start | bytes 2359296 | tf_op jit(solution)/shard_map/reduce_scatter | solution.py:208
  798.0 251.6 %reduce-scatter.17.cloned.1.call-start = ((), (), s32[]{:S(2)}) async-start(), calls=%async_computation.17 | async-start | bytes 7864320 | tf_op jit(solution)/shard_map/reduce_scatter | solution.py:180
  798.3 10.2 copy-start.15
  798.3 10.2 copy-start.33
  833.6 215.9 %copy-start.21 = (f32[2048]{0:T(1024)S(1)}, f32[2048]{0:T(1024)}, u32[]{:S(2)}) copy-start(f32[2048]{0:T(1024)} %param.23) | copy-start | bytes 24580
  833.6 215.9 %copy-start.23 = (f32[384]{0:T(512)S(1)}, f32[384]{0:T(512)}, u32[]{:S(2)}) copy-start(f32[384]{0:T(512)} %copy-done.22) | copy-start | bytes 4612
  836.4 216.0 %copy-start.31 = (f32[384]{0:T(512)S(1)}, f32[384]{0:T(512)}, u32[]{:S(2)}) copy-start(f32[384]{0:T(512)} %copy-done.30) | copy-start | bytes 4612
  836.4 216.0 %copy-start.26 = (f32[384]{0:T(512)S(1)}, f32[384]{0:T(512)}, u32[]{:S(2)}) copy-start(f32[384]{0:T(512)} %copy-done.25) | copy-start | bytes 4612
  979.6 74.4 %copy-start.27 = (f32[2048]{0:T(1024)S(1)}, f32[2048]{0:T(1024)}, u32[]{:S(2)}) copy-start(f32[2048]{0:T(1024)} %get-tuple-element.141) | copy-start | bytes 24580
  979.6 113.9 %copy-start.29 = (f32[384]{0:T(512)S(1)}, f32[384]{0:T(512)}, u32[]{:S(2)}) copy-start(f32[384]{0:T(512)} %copy-done.28) | copy-start | bytes 4612
  1049.6 2.8 copy-start.5
  1049.6 2.8 copy-start.12
  (6 other events, 8.0 us)
Sparse Core Ops, SparseCore 0:
  14.1 72.8 all-gather.4
  163.2 70.2 reduce-scatter.10
  235.3 70.1 all-gather.8
  307.7 70.1 all-gather.6
  426.8 70.1 reduce-scatter.14
  499.8 70.1 reduce-scatter.12
  579.0 70.1 all-gather.10
  651.4 89.5 reduce-scatter.26
  743.4 87.9 reduce-scatter.28
  833.5 34.0 reduce-scatter.24
  870.0 34.3 reduce-scatter.18
  906.5 34.5 reduce-scatter.22
  943.4 34.3 reduce-scatter.20
  980.6 68.8 reduce-scatter.16
where the time goes:
time: 1110 us
  waiting for transfers between devices  616 us (55%)
  matrix products  285 us (26%)
  local copies, waits for them, and re-layouts  78.1 us (7%)
  other arithmetic  71.6 us (6%)
  blocking collectives  39.5 us (4%)
  between operations  14.6 us (1%)
    all_gather x1, waiting for transfers between devices, local(): lax.all_gather(normed_attn.astype(jnp.bfloat16), 'mp', axis=0, tiled=True)  73 us
    reduce_scatter x1, waiting for transfers between devices, local(): lax.psum_scatter(attn_input_back(queries_grad, keys_grad, values_grad, qu...  70 us
    reduce_scatter x1, waiting for transfers between devices, local(): lax.psum_scatter(rows_times(context_flat, out_weight).astype(jnp.bfloat16...  69.6 us
    reduce_scatter x1, waiting for transfers between devices, local(): lax.psum_scatter(rows_times(hidden, down_weight).astype(jnp.bfloat16), 'm...  68.7 us
    all_gather x1, waiting for transfers between devices, local(): cotangent_all = lax.all_gather(out_cotangent, 'mp', axis=0, tiled=True)  66.6 us
    all_gather x1, waiting for transfers between devices, local(): lax.all_gather(normed_mlp.astype(jnp.bfloat16), 'mp', axis=0, tiled=True)  53.4 us
    dot_general x4, matrix products, rows_times_back(): lax.dot_general(left_rows, right_matrix, (((1,), (1,)), ((), ())), prefer...  51.6 us
    reduce_scatter x1, waiting for transfers between devices, local(): lax.psum_scatter(rows_times_back(pre_grad, up_weight).astype(jnp.bfloat16...  49.7 us
  transfers between devices with their start and end apart: 14, of which 12 were waited for; matrix products, arithmetic and copies ran while one was open for 25% of the time, Pallas kernels for 0%

commit v1 on v0

--- a/solution.py
+++ b/solution.py
@@ -134,7 +134,12 @@
         rows_times(hidden, down_weight).astype(jnp.bfloat16), "mp", scatter_dimension=0, tiled=True
     ).astype(jnp.float32)
     layer_output = (residual_mid + mlp_rows).astype(jnp.bfloat16)
-    cotangent_all = lax.all_gather(out_cotangent, "mp", axis=0, tiled=True)
+    ring = [out_cotangent]
+    for hop in range(3):
+        ring.append(lax.ppermute(ring[-1], "mp", [(dev, (dev + 1) % 4) for dev in range(4)]))
+    cotangent_all = jnp.roll(
+        jnp.concatenate(ring[::-1], axis=0), (lax.axis_index("mp") + 1) * ring[0].shape[0], axis=0
+    )
     down_weight_grad = jnp.einsum(
         "rf,rd->fd", hidden, cotangent_all, preferred_element_type=jnp.float32
     )

time: 1110 us -> 1160 us (1.045)
  waiting for transfers between devices: 616 us -> 648 us
  local copies, waits for them, and re-layouts: 78.1 us -> 95.3 us
    ppermute x0 -> x3, waiting for transfers between devices: none -> 153 us  [local(): lax.ppermute(ring[-1], 'mp', [(dev, (dev + 1) % 4) for dev in range(4)])]
    all_gather x1 -> x0, waiting for transfers between devices: 66.6 us -> none  [local(): cotangent_all = lax.all_gather(out_cotangent, 'mp', axis=0, tiled=True)]
    all_gather x1, waiting for transfers between devices: 53.4 us -> 0.01 us  [local(): lax.all_gather(normed_mlp.astype(jnp.bfloat16), 'mp', axis=0, tiled=True)]
    unnamed x56 -> x69, local copies, waits for them, and re-layouts: 3.2 us -> 19.3 us
  transfers between devices with their start and end apart: 14 -> 16, of which waited for: 12 -> 13; matrix products, arithmetic and copies ran while one was open for 25% -> 23% of each run, Pallas kernels for 0% -> 0%
where the time goes in v1:
time: 1160 us
  waiting for transfers between devices  648 us (56%)
  matrix products  284 us (24%)
  local copies, waits for them, and re-layouts  95.3 us (8%)
  other arithmetic  71.6 us (6%)
  blocking collectives  39.5 us (3%)
  between operations  14.5 us (1%)
    ppermute x3, waiting for transfers between devices, local(): lax.ppermute(ring[-1], 'mp', [(dev, (dev + 1) % 4) for dev in range(4)])  153 us
    all_gather x1, waiting for transfers between devices, local(): lax.all_gather(normed_attn.astype(jnp.bfloat16), 'mp', axis=0, tiled=True)  73 us
    reduce_scatter x1, waiting for transfers between devices, local(): lax.psum_scatter(rows_times(context_flat, out_weight).astype(jnp.bfloat16...  70.3 us
    reduce_scatter x1, waiting for transfers between devices, local(): lax.psum_scatter(attn_input_back(queries_grad, keys_grad, values_grad, qu...  70.1 us
    reduce_scatter x1, waiting for transfers between devices, local(): lax.psum_scatter(rows_times(hidden, down_weight).astype(jnp.bfloat16), 'm...  68.7 us
    dot_general x4, matrix products, rows_times_back(): lax.dot_general(left_rows, right_matrix, (((1,), (1,)), ((), ())), prefer...  51.7 us
    reduce_scatter x1, waiting for transfers between devices, local(): lax.psum_scatter(rows_times_back(pre_grad, up_weight).astype(jnp.bfloat16...  49.1 us
    psum x1, blocking collectives, local(): lax.psum((attn_gain_grad, mlp_gain_grad), ('dp', 'mp'))  39.5 us
  transfers between devices with their start and end apart: 16, of which 13 were waited for; matrix products, arithmetic and copies ran while one was open for 23% of the time, Pallas kernels for 0%

profile of v1, /device:TPU:0, one launch (start us, length us, event | category | flops | bytes accessed | tf_op | source)
XLA Modules:
  0.0 1158.7 jit_solution(5650380262211317874)
XLA Ops:
  14.0 73.0 %all-gather.4.cloned.1.call-done = bf16[1536,2048]{1,0:T(8,128)(2,1)} async-done(((bf16[384,2048]{1,0:T(8,128)(2,1)}), bf16[1536,2048]{1,0:T(8,128)(2,1)}) %all-gather.4.cloned.1.call-update) | async-done | bytes 6291472 | tf_op jit(solution)/shard_map/all_gather | solution.py:106
  87.0 8.0 convolution_convert_fusion.11
  95.0 3.7 reshape.216
  101.6 7.3 fusion.68
  115.3 7.3 convolution_convert_fusion.12
  127.7 28.2 %while.26 = (s32[]{:T(128)}, bf16[2,768,4,128]{3,2,1,0:T(4,128)(2,1)}, f32[2,4,768]{2,1,0:T(4,128)S(1)}, bf16[2,768,4,128]{3,2,1,0:T(4,128)(2,1)}, s32[2,768]{1,...) while((s32[]{:T(128)}, ...), condition=%wide.region_5.6_spmd, body=%wide.region_2.5_spmd.sunk | while | flops 1231352832 | bytes 43362440 | solution.py:119
  135.5 3.6 fusion.142
  155.9 7.0 convolution_convert_fusion.6
  163.0 70.3 %reduce-scatter.11.cloned.1.call-done = bf16[384,2048]{1,0:T(8,128)(2,1)} async-done(((bf16[1536,2048]{1,0:T(8,128)(2,1)}), bf16[384,2048]{1,0:T(8,128)(2,1)}) %reduce-scatter.11.cloned.1.call-update) | async-done | bytes 1572880 | tf_op jit(solution)/shard_map/reduce_scatter | solution.py:121
  240.1 53.7 %collective-permute-done = bf16[384,2048]{1,0:T(8,128)(2,1)S(1)} collective-permute-done((bf16[384,2048]{1,0:T(8,128)(2,1)}, bf16[384,2048]{1,0:T(8,128)(2,1)S(1)}, u32[]{:S(2)}, u32[]{:S(2)}) %collective-permute-start) | collective-permute-done | bytes 1572896 | tf_op jit(solution)/shard_map/ppermute | solution.py:139
  297.0 63.4 %collective-permute-done.1 = bf16[384,2048]{1,0:T(8,128)(2,1)} collective-permute-done((bf16[384,2048]{1,0:T(8,128)(2,1)S(1)}, bf16[384,2048]{1,0:T(8,128)(2,1)}, u32[]{:S(2)}, u32[]{:S(2)}) %collective-permute-start.1) | collective-permute-done | bytes 1572896 | tf_op jit(solution)/shard_map/ppermute | solution.py:139
  360.8 36.2 %collective-permute-done.2 = bf16[384,2048]{1,0:T(8,128)(2,1)} collective-permute-done((bf16[384,2048]{1,0:T(8,128)(2,1)}, bf16[384,2048]{1,0:T(8,128)(2,1)}, u32[]{:S(2)}, u32[]{:S(2)}) %collective-permute-start.2) | collective-permute-done | bytes 1572896 | tf_op jit(solution)/shard_map/ppermute | solution.py:139
  413.2 18.9 %fusion.96 = f32[1536,2048]{1,0:T(8,128)} fusion(bf16[1536,2048]{1,0:T(8,128)(2,1)} %all-gather.6.cloned.1.call-done, bf16[2048,2048]{1,0:T(8,128)(2,1)} %param.21), kind=kOutput, calls=%fused_computation.159 | convolution fusion | flops 12884901888 | bytes 27262976 | tf_op jit(solution)/shard_map/dot_general | solution.py:130
  432.1 29.0 %fusion.48 = bf16[1536,2048]{1,0:T(8,128)(2,1)} fusion(f32[1536,2048]{1,0:T(8,128)} %fusion.96, bf16[2048,2048]{1,0:T(8,128)(2,1)} %param.22, bf16[3072,2048]{1,0:T(8,128)(2,1)} %constant_dynamic-update-slice_fusion.4, s32[]{:T(128)S(6)} %select_n.21), kind=kOutput, calls=%fused_computation.68 | convolution fusion | flops 12947816448 | bytes 33554436 | tf_op jit(solution)/shard_map/dot_general | solution.py:146
  461.1 19.1 %convolution_convert_fusion.4 = bf16[1536,2048]{1,0:T(8,128)(2,1)} fusion(bf16[1536,2048]{1,0:T(8,128)(2,1)} %fusion.48, bf16[2048,2048]{1,0:T(8,128)(2,1)} %param.21), kind=kOutput, calls=%fused_computation.73 | convolution fusion | flops 12888047616 | bytes 20971520 | tf_op jit(solution)/shard_map/dot_general | solution.py:33
  480.3 20.5 %convolution_convert_fusion.5 = bf16[1536,2048]{1,0:T(8,128)(2,1)} fusion(bf16[2048,2048]{1,0:T(8,128)(2,1)} %param.22, f32[1536,2048]{1,0:T(8,128)} %fusion.96), kind=kOutput, calls=%fused_computation.74 | convolution fusion | flops 12916359168 | bytes 27262976 | tf_op jit(solution)/shard_map/dot_general | solution.py:29
  500.9 49.1 %reduce-scatter.15.cloned.1.call-done = bf16[384,2048]{1,0:T(8,128)(2,1)} async-done(((bf16[1536,2048]{1,0:T(8,128)(2,1)}), bf16[384,2048]{1,0:T(8,128)(2,1)}) %reduce-scatter.15.cloned.1.call-update) | async-done | bytes 1572880 | tf_op jit(solution)/shard_map/reduce_scatter | solution.py:153
  550.1 4.4 fusion.64
  554.4 68.7 %reduce-scatter.13.cloned.1.call-done = bf16[384,2048]{1,0:T(8,128)(2,1)} async-done(((bf16[1536,2048]{1,0:T(8,128)(2,1)}), bf16[384,2048]{1,0:T(8,128)(2,1)}) %reduce-scatter.13.cloned.1.call-update) | async-done | bytes 1572880 | tf_op jit(solution)/shard_map/reduce_scatter | solution.py:133
  623.1 5.5 fusion.95
  632.0 23.9 %convolution_convert_fusion.2 = bf16[2048,2048]{1,0:T(8,128)(2,1)} fusion(bf16[3072,2048]{1,0:T(8,128)(2,1)} %constant_dynamic-update-slice_fusion.4, s32[]{:T(128)S(6)} %select_n.21, f32[1536,2048]{1,0:T(8,128)} %fusion.96), kind=kOutput, calls=%fused_computation.71 | convolution fusion | flops 12917407744 | bytes 27262980 | tf_op jit(solution)/shard_map/rf,rd->fd/dot_general | solution.py:143
  655.9 19.7 %convolution_convert_fusion.3 = bf16[2048,2048]{1,0:T(8,128)(2,1)} fusion(bf16[1536,2048]{1,0:T(8,128)(2,1)} %all-gather.6.cloned.1.call-done, bf16[1536,2048]{1,0:T(8,128)(2,1)} %fusion.48), kind=kOutput, calls=%fused_computation.72 | convolution fusion | flops 12889096192 | bytes 20971520 | tf_op jit(solution)/shard_map/rd,rf->df/dot_general | solution.py:150
  675.7 26.5 %all-gather.8.cloned.1.call-done = bf16[1536,2048]{1,0:T(8,128)(2,1)} async-done(((bf16[384,2048]{1,0:T(8,128)(2,1)}), bf16[1536,2048]{1,0:T(8,128)(2,1)}) %all-gather.8.cloned.1.call-update) | async-done | bytes 6291472 | tf_op jit(solution)/shard_map/all_gather | solution.py:161
  702.2 7.4 convolution_convert_fusion.10
  709.6 3.7 reshape.218
  713.3 8.0 convolution_convert_fusion.7
  726.1 99.5 %while.27 = (s32[]{:T(128)}, bf16[2,768,4,128]{3,2,1,0:T(4,128)(2,1)}, bf16[2,768,4,128]{3,2,1,0:T(4,128)(2,1)}, bf16[2,768,4,128]{3,2,1,0:T(4,128)(2,1)}, bf16[...) while((s32[]{:T(128)}, ...), condition=%wide.region_15.16_spmd, body=%wide.region_13.15_spmd.sunk | while | flops 3051156480 | bytes 169179440 | solution.py:168
  732.0 3.6 copy-done.1
  741.4 8.0 multiply_reduce_fusion.3
  749.4 10.9 multiply_convert_fusion.7
  760.3 4.4 fusion.154
  781.2 3.6 copy-done.1
  790.5 8.1 multiply_reduce_fusion.3
  798.6 11.5 multiply_convert_fusion.7
  810.1 4.5 fusion.154
  825.5 8.1 multiply_convert_fusion.2
  833.7 8.0 convolution_convert_fusion.8
  841.8 8.1 convolution_convert_fusion.9
  850.3 10.3 fusion.77
  860.5 6.5 fusion.74
  867.0 15.8 %add_convert_fusion = bf16[1536,2048]{1,0:T(8,128)(2,1)} fusion(f32[1536,2048]{1,0:T(8,128)} %fusion.74, f32[1536,2048]{1,0:T(8,128)} %fusion.77, bf16[2048,512]{1,0:T(8,128)(2,1)} %param.17, bf16[192,8,4,128]{3,2,1,0:T(4,128)(2,1)} %bitcast.145), kind=kOutput, calls=%fused_computation.69 | convolution fusion | flops 3233808384 | bytes 35127296 | tf_op jit(solution)/shard_map/dot_general | solution.py:33
  888.4 32.5 %reduce-scatter.25.cloned.1.call-done = bf16[512,256]{1,0:T(8,128)(2,1)} async-done(((bf16[512,2048]{1,0:T(8,128)(2,1)}), bf16[512,256]{1,0:T(8,128)(2,1)}) %reduce-scatter.25.cloned.1.call-update) | async-done | bytes 262160 | tf_op jit(solution)/shard_map/reduce_scatter | solution.py:219
  922.7 34.7 %reduce-scatter.19.cloned.1.call-done = bf16[256,512]{1,0:T(8,128)(2,1)} async-done(((bf16[2048,512]{1,0:T(8,128)(2,1)}), bf16[256,512]{1,0:T(8,128)(2,1)}) %reduce-scatter.19.cloned.1.call-update) | async-done | bytes 262160 | tf_op jit(solution)/shard_map/reduce_scatter | solution.py:210
  959.2 35.0 %reduce-scatter.23.cloned.1.call-done = bf16[256,512]{1,0:T(8,128)(2,1)} async-done(((bf16[2048,512]{1,0:T(8,128)(2,1)}), bf16[256,512]{1,0:T(8,128)(2,1)}) %reduce-scatter.23.cloned.1.call-update) | async-done | bytes 262160 | tf_op jit(solution)/shard_map/reduce_scatter | solution.py:216
  996.0 34.8 %reduce-scatter.21.cloned.1.call-done = bf16[256,512]{1,0:T(8,128)(2,1)} async-done(((bf16[2048,512]{1,0:T(8,128)(2,1)}), bf16[256,512]{1,0:T(8,128)(2,1)}) %reduce-scatter.21.cloned.1.call-update) | async-done | bytes 262160 | tf_op jit(solution)/shard_map/reduce_scatter | solution.py:213
  1032.6 70.1 %reduce-scatter.17.cloned.1.call-done = bf16[384,2048]{1,0:T(8,128)(2,1)} async-done(((bf16[1536,2048]{1,0:T(8,128)(2,1)}), bf16[384,2048]{1,0:T(8,128)(2,1)}) %reduce-scatter.17.cloned.1.call-update) | async-done | bytes 1572880 | tf_op jit(solution)/shard_map/reduce_scatter | solution.py:185
  1107.1 39.5 %all-reduce = (f32[2048]{0:T(1024)}, f32[2048]{0:T(1024)}) all-reduce(f32[2048]{0:T(1024)S(1)} %get-tuple-element.143, f32[2048]{0:T(1024)S(1)} %copy-done.30), channel_id=1, replica_groups=mesh['dp'=8,'mp'=4] {'dp','mp'}, use_global_device_ids=true, to_apply=%region_26.27 | all-reduce | flops 4096 | bytes 32768 | tf_op jit(solution)/shard_map/psum | solution.py:201
  1146.6 5.1 add_add_fusion.2
  (201 shorter events, 142.5 us)
Async XLA Ops:
  7.2 148.7 %copy-start = (bf16[512,2048]{1,0:T(8,128)(2,1)S(1)}, bf16[512,2048]{1,0:T(8,128)(2,1)}, u32[]{:S(2)}) copy-start(bf16[512,2048]{1,0:T(8,128)(2,1)} %param.20) | copy-start | bytes 6291460
  7.2 5.1 copy-start.23
  7.2 79.8 %all-gather.4.cloned.1.call-start = ((), (), s32[]{:S(2)}) async-start(), calls=%async_computation.10 | async-start | bytes 7864320 | tf_op jit(solution)/shard_map/all_gather | solution.py:106
  7.2 5.0 copy-start.3
  14.0 219.3 %reduce-scatter.11.cloned.1.call-start = ((), (), s32[]{:S(2)}) async-start(), calls=%async_computation.11 | async-start | bytes 7864320 | tf_op jit(solution)/shard_map/reduce_scatter | solution.py:121
  98.7 2.9 copy-start.17
  112.4 2.9 copy-start.35
  122.6 5.1 copy-start.21
  155.9 7.0 copy-start.19
  162.9 73.9 %copy-start.27 = (f32[2048]{0:T(1024)S(1)}, f32[2048]{0:T(1024)}, u32[]{:S(2)}) copy-start(f32[2048]{0:T(1024)} %param.24) | copy-start | bytes 24580
  162.9 250.3 %all-gather.6.cloned.1.call-start = ((), (), s32[]{:S(2)}) async-start(), calls=%async_computation.12 | async-start | bytes 7864320 | tf_op jit(solution)/shard_map/all_gather | solution.py:129
  238.7 311.4 %reduce-scatter.15.cloned.1.call-start = ((), (), s32[]{:S(2)}) async-start(), calls=%async_computation.14 | async-start | bytes 7864320 | tf_op jit(solution)/shard_map/reduce_scatter | solution.py:153
  238.7 55.0 %collective-permute-start = (bf16[384,2048]{1,0:T(8,128)(2,1)}, bf16[384,2048]{1,0:T(8,128)(2,1)S(1)}, u32[]{:S(2)}, u32[]{:S(2)}) collective-permute-start(bf16[384,2048]{1,0:T(8,128)(2,1)} %param.25), channel_id=1, source_target_pairs={{0,1},{1,2},{2,3},{3,0},{4,5},{5,6},{6,7},{7,4},{8,9},{9,10},{10,1... | collective-permute-start | bytes 4718600 | tf_op jit(solution)/shard_map/ppermute | solution.py:139
  294.9 65.5 %collective-permute-start.1 = (bf16[384,2048]{1,0:T(8,128)(2,1)S(1)}, bf16[384,2048]{1,0:T(8,128)(2,1)}, u32[]{:S(2)}, u32[]{:S(2)}) collective-permute-start(bf16[384,2048]{1,0:T(8,128)(2,1)S(1)} %collective-permute-done), channel_id=1, source_target_pairs={{0,1},{1,2},{2,3},{3,0},{4,5},{5,6},{6,7},{7,4},{8,9},{9,10},{10,1... | collective-permute-start | bytes 4718600 | tf_op jit(solution)/shard_map/ppermute | solution.py:139
  360.4 36.7 %collective-permute-start.2 = (bf16[384,2048]{1,0:T(8,128)(2,1)}, bf16[384,2048]{1,0:T(8,128)(2,1)}, u32[]{:S(2)}, u32[]{:S(2)}) collective-permute-start(bf16[384,2048]{1,0:T(8,128)(2,1)} %collective-permute-done.1), channel_id=1, source_target_pairs={{0,1},{1,2},{2,3},{3,0},{4,5},{5,6},{6,7},{7,4},{8,9},{9,10},{10,1... | collective-permute-start | bytes 4718600 | tf_op jit(solution)/shard_map/ppermute | solution.py:139
  360.8 41.8 %copy-start.16 = (bf16[384,2048]{1,0:T(8,128)(2,1)S(1)}, bf16[384,2048]{1,0:T(8,128)(2,1)}, u32[]{:S(2)}) copy-start(bf16[384,2048]{1,0:T(8,128)(2,1)} %copy-done.15) | copy-start | bytes 4718596
  399.8 4.1 copy-start.11
  480.3 142.8 %reduce-scatter.13.cloned.1.call-start = ((), (), s32[]{:S(2)}) async-start(), calls=%async_computation.13 | async-start | bytes 7864320 | tf_op jit(solution)/shard_map/reduce_scatter | solution.py:133
  500.9 201.3 %all-gather.8.cloned.1.call-start = ((), (), s32[]{:S(2)}) async-start(), calls=%async_computation.15 | async-start | bytes 7864320 | tf_op jit(solution)/shard_map/all_gather | solution.py:161
  623.1 7.2 copy-start.12
  631.9 251.0 %reduce-scatter.29.cloned.1.call-start = ((), (), s32[]{:S(2)}) async-start(), calls=%async_computation.22 | async-start | bytes 9437184 | tf_op jit(solution)/shard_map/reduce_scatter | solution.py:225
  655.9 229.7 %reduce-scatter.27.cloned.1.call-start = ((), (), s32[]{:S(2)}) async-start(), calls=%async_computation.21 | async-start | bytes 9437184 | tf_op jit(solution)/shard_map/reduce_scatter | solution.py:222
  675.7 245.2 %reduce-scatter.25.cloned.1.call-start = ((), (), s32[]{:S(2)}) async-start(), calls=%async_computation.20 | async-start | bytes 2359296 | tf_op jit(solution)/shard_map/reduce_scatter | solution.py:219
  721.3 4.7 copy-start.20
  721.3 4.7 copy-start.22
  721.3 236.0 %reduce-scatter.19.cloned.1.call-start = ((), (), s32[]{:S(2)}) async-start(), calls=%async_computation.17 | async-start | bytes 2359296 | tf_op jit(solution)/shard_map/reduce_scatter | solution.py:210
  726.2 4.4 copy-start.6
  726.2 4.4 copy-start.8
  732.0 3.6 copy-start.1
  760.3 4.4 copy-start.2
  760.3 4.6 copy-start.7
  775.5 4.3 copy-start.6
  775.5 4.3 copy-start.8
  781.2 3.6 copy-start.1
  810.1 4.5 copy-start.2
  810.1 4.6 copy-start.7
  833.6 160.5 %reduce-scatter.23.cloned.1.call-start = ((), (), s32[]{:S(2)}) async-start(), calls=%async_computation.19 | async-start | bytes 2359296 | tf_op jit(solution)/shard_map/reduce_scatter | solution.py:216
  841.7 189.0 %reduce-scatter.21.cloned.1.call-start = ((), (), s32[]{:S(2)}) async-start(), calls=%async_computation.18 | async-start | bytes 2359296 | tf_op jit(solution)/shard_map/reduce_scatter | solution.py:213
  849.9 252.7 %reduce-scatter.17.cloned.1.call-start = ((), (), s32[]{:S(2)}) async-start(), calls=%async_computation.16 | async-start | bytes 7864320 | tf_op jit(solution)/shard_map/reduce_scatter | solution.py:185
  850.3 10.3 copy-start.18
  850.3 10.3 copy-start.36
  885.6 217.0 %copy-start.24 = (f32[2048]{0:T(1024)S(1)}, f32[2048]{0:T(1024)}, u32[]{:S(2)}) copy-start(f32[2048]{0:T(1024)} %param.23) | copy-start | bytes 24580
  885.6 217.0 %copy-start.26 = (f32[384]{0:T(512)S(1)}, f32[384]{0:T(512)}, u32[]{:S(2)}) copy-start(f32[384]{0:T(512)} %copy-done.25) | copy-start | bytes 4612
  888.4 217.0 %copy-start.34 = (f32[384]{0:T(512)S(1)}, f32[384]{0:T(512)}, u32[]{:S(2)}) copy-start(f32[384]{0:T(512)} %copy-done.33) | copy-start | bytes 4612
  888.4 217.1 %copy-start.29 = (f32[384]{0:T(512)S(1)}, f32[384]{0:T(512)}, u32[]{:S(2)}) copy-start(f32[384]{0:T(512)} %copy-done.28) | copy-start | bytes 4612
  1032.5 74.5 %copy-start.30 = (f32[2048]{0:T(1024)S(1)}, f32[2048]{0:T(1024)}, u32[]{:S(2)}) copy-start(f32[2048]{0:T(1024)} %get-tuple-element.141) | copy-start | bytes 24580
  1032.5 114.0 %copy-start.32 = (f32[384]{0:T(512)S(1)}, f32[384]{0:T(512)}, u32[]{:S(2)}) copy-start(f32[384]{0:T(512)} %copy-done.31) | copy-start | bytes 4612
  1102.6 2.8 copy-start.14
  (11 other events, 19.9 us)
Sparse Core Ops, SparseCore 0:
  14.1 72.8 all-gather.3
  163.0 70.1 reduce-scatter.10
  238.8 117.2 all-gather.5
  480.4 69.6 reduce-scatter.14
  552.9 70.1 reduce-scatter.12
  632.0 70.1 all-gather.7
  704.5 89.5 reduce-scatter.28
  796.4 87.9 reduce-scatter.26
  886.7 34.0 reduce-scatter.24
  923.0 34.3 reduce-scatter.18
  959.7 34.4 reduce-scatter.22
  996.3 34.3 reduce-scatter.20
  1033.7 68.8 reduce-scatter.16
